TPU v7x, 256 devices: a whole 4x4x8 slice. The times are simulated.
256 devices in a mesh: phase: 16 (over y_hi, x, core), chan: 16 (over z, y_lo).
Axes of the slice: x: 4, y: 4 (y_hi: 2, y_lo: 2; y = y_hi * 2 + y_lo), z: 8, core: 2. Of those that a mesh axis runs over, the one named last changes fastest.
Arguments:
- frames: bfloat16 [64, 32, 2048], P(None, 'phase', 'chan'), may hold values from -6 to 6
- temporal_taps: float32 [4, 3, 64], replicated, may hold values from -3 to 3
- conv_weights: bfloat16 [4, 64, 27, 2, 64], P(None, None, None, None, 'chan'), may hold values from -0.15625 to 0.15625
- cotangent: bfloat16 [64, 32, 2048], P(None, 'phase', 'chan'), may hold values from -16 to 16
Outputs:
- final_frames: bfloat16 [64, 32, 2048], P(None, 'phase', 'chan')
- grad_frames: bfloat16 [64, 32, 2048], P(None, 'phase', 'chan')
- grad_taps: float32 [4, 3, 64], replicated
- grad_weights: float32 [4, 64, 27, 2, 64], P(None, None, None, None, 'chan')
All inputs are finite; a program needn't handle non-finite values.
Results may differ from a plain program's by a relative error of at most 0.025.
Values may be sent and summed in bfloat16 or wider, within the bound.
No kernel may reach another device: no remote copies, remote signals or barrier semaphores. Data moves between devices by JAX's collectives and lax.ppermute only.
A program may use at most 64 MiB of HBM per device.

v0:
```python
import jax
import jax.numpy as jnp
from jax import lax
from jax.sharding import PartitionSpec as P

BLOCKS = 4
SY = 8
SZ = 16
cell_offsets = [
    (kernel_pos // 9 - 1, kernel_pos // 3 % 3 - 1, kernel_pos % 3 - 1) for kernel_pos in range(27)
]


def shifted(block, axis, distance):
    devices = range(lax.axis_size(axis))
    route = [((i - distance) % len(devices), i) for i in devices]
    return lax.ppermute(block, axis, route)


def padded_2(cells, sides, width):
    for axis, dim in sides:
        count = lax.axis_size(axis)
        ends = count - 1
        head = lax.slice_in_dim(cells, 0, width, axis=dim)
        tail = lax.slice_in_dim(cells, cells.shape[dim] - width, cells.shape[dim], axis=dim)
        cells = jnp.concatenate(
            [
                lax.ppermute(tail, axis, [(i, (i + 1) % count) for i in range(ends)]),
                cells,
                lax.ppermute(head, axis, [((i + 1) % count, i) for i in range(ends)]),
            ],
            axis=dim,
        )
    return cells


def within_plane(source, step_y, step_z):
    cell_count = source.shape[-1]
    last_dim = source.ndim - 1
    margin = SZ + 1
    moved = step_y * SZ + step_z
    padded = jnp.pad(source, [(0, 0)] * last_dim + [(margin, margin)])
    window = lax.slice_in_dim(padded, margin + moved, margin + moved + cell_count, axis=last_dim)
    places = jnp.arange(cell_count, dtype=jnp.int32)
    coord_y = places // SZ + step_y
    coord_z = places % SZ + step_z
    inside = (coord_y >= 0) & (coord_y < SY) & (coord_z >= 0) & (coord_z < SZ)
    return jnp.where(inside, window, jnp.zeros_like(window))


def shifted_cells(rimmed, step_x, step_y, step_z):
    planes = rimmed.shape[-2] - 2
    rows = lax.slice_in_dim(rimmed, 1 + step_x, 1 + step_x + planes, axis=rimmed.ndim - 2)
    moved = within_plane(rows, step_y, step_z)
    return moved.reshape(moved.shape[:-2] + (planes * moved.shape[-1],))


def offset_stack(rimmed, first, count, sign):
    picked = cell_offsets[first : first + count]
    return jnp.stack(
        [
            shifted_cells(rimmed, sign * offset[0], sign * offset[1], sign * offset[2])
            for offset in picked
        ],
        axis=1,
    )


def back_block(source, hops):
    if hops == 0:
        return source
    return shifted(source, "phase", hops)


def next_block(source, hops):
    if hops == 0:
        return source
    return shifted(source, "phase", -hops)


def neighbours(source, reach):
    phase_rows = source.shape[1]
    hops, rest = divmod(reach, phase_rows)
    if rest == 0:
        return (back_block(source, hops), next_block(source, hops))
    joined = jnp.concatenate([back_block(source, hops + 1), back_block(source, hops)], axis=1)
    behind = joined[:, phase_rows - rest : 2 * phase_rows - rest]
    joined = jnp.concatenate([next_block(source, hops), next_block(source, hops + 1)], axis=1)
    ahead = joined[:, rest : rest + phase_rows]
    return (behind, ahead)


def per_device(frames, temporal_taps, conv_weights, cotangent):
    chans, phase_rows, cell_count = frames.shape
    plane_cells = SY * SZ
    planes = cell_count // plane_cells
    state = frames
    saved = []
    for block_num in range(BLOCKS):
        reach = 2**block_num
        behind, ahead = neighbours(state, reach)
        tap_rows = temporal_taps[block_num][:, :, None, None]
        mixed = (
            tap_rows[0] * behind.astype(jnp.float32)
            + tap_rows[1] * state.astype(jnp.float32)
            + tap_rows[2] * ahead.astype(jnp.float32)
        ).astype(jnp.bfloat16)
        rimmed = padded_2(mixed.reshape(chans, phase_rows, planes, plane_cells), (("chan", 2),), 1)
        kernel = lax.all_gather(conv_weights[block_num], "chan", axis=3, tiled=True)
        conv_out = jnp.zeros((chans, 2, phase_rows, cell_count), jnp.float32)
        for first in range(0, 27, 9):
            group = offset_stack(rimmed, first, 9, 1)
            conv_out = conv_out + jnp.einsum(
                "ikpv,ikgo->ogpv",
                group,
                kernel[:, first : first + 9],
                preferred_element_type=jnp.float32,
            )
        value_part = conv_out[:, 0]
        gate_sig = jax.nn.sigmoid(conv_out[:, 1])
        saved.append((state, behind, ahead, rimmed, kernel, value_part, gate_sig))
        state = (state.astype(jnp.float32) + value_part * gate_sig).astype(jnp.bfloat16)
    grad_state = cotangent
    weight_grads = [None] * BLOCKS
    tap_grads = [None] * BLOCKS
    for block_num in reversed(range(BLOCKS)):
        reach = 2**block_num
        prior, behind, ahead, rimmed, kernel, value_part, gate_sig = saved[block_num]
        tap_rows = temporal_taps[block_num][:, :, None, None]
        grad_y = grad_state.astype(jnp.float32)
        grad_z = jnp.stack(
            [grad_y * gate_sig, grad_y * value_part * gate_sig * (1.0 - gate_sig)], axis=1
        ).astype(jnp.bfloat16)
        rim_grad = padded_2(
            grad_z.reshape(chans, 2, phase_rows, planes, plane_cells), (("chan", 3),), 1
        )
        grad_mix = jnp.zeros((chans, phase_rows, cell_count), jnp.float32)
        for first in range(0, 27, 3):
            group = offset_stack(rim_grad, first, 3, -1)
            grad_mix = grad_mix + jnp.einsum(
                "okgpv,ikgo->ipv",
                group,
                kernel[:, first : first + 3],
                preferred_element_type=jnp.float32,
            )
        kernel_parts = []
        for first in range(0, 27, 9):
            group = offset_stack(rimmed, first, 9, 1)
            kernel_parts.append(
                jnp.einsum("ikpv,ogpv->ikgo", group, grad_z, preferred_element_type=jnp.float32)
            )
        grad_kernel = jnp.concatenate(kernel_parts, axis=1)
        grad_tap = jnp.stack(
            [
                jnp.sum(grad_mix * behind.astype(jnp.float32), axis=(1, 2)),
                jnp.sum(grad_mix * prior.astype(jnp.float32), axis=(1, 2)),
                jnp.sum(grad_mix * ahead.astype(jnp.float32), axis=(1, 2)),
            ]
        )
        grad_low = grad_mix.astype(jnp.bfloat16)
        back_mix, ahead_mix = neighbours(grad_low, reach)
        grad_state = (
            grad_y
            + tap_rows[0] * ahead_mix.astype(jnp.float32)
            + tap_rows[1] * grad_low.astype(jnp.float32)
            + tap_rows[2] * back_mix.astype(jnp.float32)
        ).astype(jnp.bfloat16)
        kernel_piece = lax.psum_scatter(
            grad_kernel.astype(jnp.bfloat16), "chan", scatter_dimension=3, tiled=True
        )
        grad_kernel = lax.psum(kernel_piece, "phase").astype(jnp.float32)
        weight_grads[block_num] = grad_kernel
        tap_grads[block_num] = grad_tap
    grad_weights = jnp.stack(weight_grads)
    grad_taps = lax.psum(jnp.stack(tap_grads), ("phase", "chan"))
    return (state, grad_state, grad_taps, grad_weights)


def solution(mesh):
    in_specs = (
        P(None, "phase", "chan"),
        P(),
        P(None, None, None, None, "chan"),
        P(None, "phase", "chan"),
    )
    out_specs = (
        P(None, "phase", "chan"),
        P(None, "phase", "chan"),
        P(),
        P(None, None, None, None, "chan"),
    )
    return jax.shard_map(
        per_device, mesh=mesh, in_specs=in_specs, out_specs=out_specs, check_vma=False
    )
```

profile of v0, /device:TPU:7, one launch (start us, length us, event | category | flops | bytes accessed | tf_op | source)
XLA Modules:
  0.0 648.9 jit_solution(4640616665763876973)
XLA Ops:
  8.0 3.4 collective-permute-start
  12.5 34.2 %all-gather = bf16[1,64,27,2,64]{1,3,2,0,4:T(2,128)(2,1)S(1)} all-gather(bf16[1,64,27,2,4]{1,3,2,0,4:T(2,128)(2,1)S(1)} %copy.558), channel_id=2, replica_groups=mesh['phase'=16,'chan'=16] {'chan'}, dimensions={4}, use_global_device_ids=true | all-gather | bytes 470016 | tf_op jit(solution)/shard_map/all_gather | solution.py:109
  49.0 4.0 collective-permute-start.2
  56.6 13.0 %collective-permute-start.4 = (bf16[64,2,128]{2,0,1:T(8,128)(2,1)S(1)}, bf16[64,2,128]{2,0,1:T(8,128)(2,1)S(1)}, u32[]{:S(2)}, u32[]{:S(2)}) collective-permute-start(bf16[64,2,128]{2,0,1:T(8,128)(2,1)S(1)} %fusion.164), channel_id=1, source_target_pairs={{240,0},{0,16},{16,32},{32,48},{48,64},{64,80},{80,96},{96,112},{1... | collective-permute-start | bytes 98312 | tf_op jit(solution)/shard_map/ppermute | solution.py:17
  70.7 5.9 collective-permute-done.5
  77.2 2.9 collective-permute-start.6
  81.4 31.7 %all-gather.1 = bf16[1,64,27,2,64]{1,3,2,0,4:T(2,128)(2,1)S(1)} all-gather(bf16[1,64,27,2,4]{1,3,2,0,4:T(2,128)(2,1)S(1)} %copy.559), channel_id=3, replica_groups=mesh['phase'=16,'chan'=16] {'chan'}, dimensions={4}, use_global_device_ids=true | all-gather | bytes 470016 | tf_op jit(solution)/shard_map/all_gather | solution.py:109
  115.8 1.5 collective-permute-start.9
  118.6 3.7 collective-permute-done.9
  122.9 2.8 collective-permute-start.10
  127.0 33.8 %all-gather.2 = bf16[1,64,27,2,64]{1,3,2,0,4:T(2,128)(2,1)S(1)} all-gather(bf16[1,64,27,2,4]{1,3,2,0,4:T(2,128)(2,1)S(1)} %copy.560), channel_id=4, replica_groups=mesh['phase'=16,'chan'=16] {'chan'}, dimensions={4}, use_global_device_ids=true | all-gather | bytes 470016 | tf_op jit(solution)/shard_map/all_gather | solution.py:109
  163.5 3.0 collective-permute-start.13
  167.7 2.5 collective-permute-done.13
  170.8 2.2 collective-permute-start.14
  174.4 30.8 %all-gather.3 = bf16[1,64,27,2,64]{1,3,2,0,4:T(2,128)(2,1)S(1)} all-gather(bf16[1,64,27,2,4]{1,3,2,0,4:T(2,128)(2,1)S(1)} %copy.561), channel_id=5, replica_groups=mesh['phase'=16,'chan'=16] {'chan'}, dimensions={4}, use_global_device_ids=true | all-gather | bytes 470016 | tf_op jit(solution)/shard_map/all_gather | solution.py:109
  214.5 4.0 collective-permute-start.17
  225.3 2.3 collective-permute-start.18
  228.9 3.1 collective-permute-done.18
  232.1 1.4 collective-permute-start.20
  236.0 4.0 collective-permute-start.21
  247.8 4.1 collective-permute-done.22
  253.8 4.6 collective-permute-start.25
  264.3 26.8 %collective-permute-start.27 = (bf16[64,2,128]{2,0,1:T(8,128)(2,1)S(1)}, bf16[64,2,128]{2,0,1:T(8,128)(2,1)S(1)}, u32[]{:S(2)}, u32[]{:S(2)}) collective-permute-start(bf16[64,2,128]{2,0,1:T(8,128)(2,1)S(1)} %get-tuple-element.46), channel_id=1, source_target_pairs={{240,0},{0,16},{16,32},{32,48},{48,64},{64,80},{80,96},{96,112},{1... | collective-permute-start | bytes 98312 | tf_op jit(solution)/shard_map/ppermute | solution.py:17
  292.1 5.9 collective-permute-done.26
  299.9 4.9 collective-permute-start.29
  313.8 85.8 %psum.35 = f32[4,3,64]{2,1,0:T(4,128)S(1)} all-reduce(f32[4,3,64]{2,1,0:T(4,128)S(1)} %pad_maximum_fusion.48), channel_id=1, replica_groups=mesh['phase'=16,'chan'=16] {'phase','chan'}, use_global_device_ids=true, to_apply=%region_12.13 | all-reduce | flops 768 | bytes 6144 | tf_op jit(solution)/shard_map/psum | solution.py:175
  400.2 91.4 %all-reduce.33.cloned.1.call-done = (bf16[64,27,2,64]{0,3,1,2:T(8,128)(2,1)}, bf16[64,27,2,64]{0,3,1,2:T(8,128)(2,1)}, bf16[64,27,2,64]{0,3,1,2:T(8,128)(2,1)}, bf16[64,27,2,64]{0,3,1,2:T(8,128)(2,1)}) async-done(((bf16[64,27,2,64]{0,3,1,2:T(8,128)(2,1)}, bf16[64,27,2,64]{0,3,1,2:T(8,128)(2,1)}, bf16[64,27,2,64]{0,3,1,2:T(8,128)(2,1)}, bf16[64,27,2,64]{0,3,1,2:T(8,128)(2,1)}), ...) | async-done | bytes 1769488
  491.6 1.5 dynamic-slice_bitcast_fusion
  493.1 1.5 dynamic-slice_bitcast_fusion.1
  494.7 1.6 dynamic-slice_bitcast_fusion.2
  496.2 1.5 dynamic-slice_bitcast_fusion.3
  499.2 140.9 %all-reduce.35.cloned.1.call-done = (bf16[1,64,27,2,4]{1,4,2,3,0:T(4,128)(2,1)}, bf16[1,64,27,2,4]{1,4,2,3,0:T(4,128)(2,1)}, bf16[1,64,27,2,4]{1,4,2,3,0:T(4,128)(2,1)}, bf16[1,64,27,2,4]{1,4,2,3,0:T(4,128)(2,1)}) async-done(((bf16[1,64,27,2,4]{1,4,2,3,0:T(4,128)(2,1)}, bf16[1,64,27,2,4]{1,4,2,3,0:T(4,128)(2,1)}, bf16[1,64,27,2,4]{1,4,2,3,0:T(4,128)(2,1)}, bf16[1,64,27,2,4]{1,4,2,3,0:T(4,128)(2,1)}), ...) | async-done | bytes 110608 | tf_op jit(solution)/shard_map/psum | solution.py:171
  (389 shorter events, 71.5 us)
Async XLA Ops:
  7.2 484.4 %all-reduce.33.cloned.1.call-start = ((), (), s32[]{:S(2)}) async-start(), calls=%async_computation | async-start | bytes 7077888
  8.0 38.9 %collective-permute-start = (bf16[64,2,128]{2,0,1:T(8,128)(2,1)S(1)}, bf16[64,2,128]{2,0,1:T(8,128)(2,1)S(1)}, u32[]{:S(2)}, u32[]{:S(2)}) collective-permute-start(bf16[64,2,128]{2,0,1:T(8,128)(2,1)S(1)} %copy.143), channel_id=1, source_target_pairs={{240,0},{0,16},{16,32},{32,48},{48,64},{64,80},{80,96},{96,112},{1... | collective-permute-start | bytes 98312 | tf_op jit(solution)/shard_map/ppermute | solution.py:17
  11.4 35.5 %collective-permute-start.1 = (bf16[64,2,128]{2,0,1:T(8,128)(2,1)S(1)}, bf16[64,2,128]{2,0,1:T(8,128)(2,1)S(1)}, u32[]{:S(2)}, u32[]{:S(2)}) collective-permute-start(bf16[64,2,128]{2,0,1:T(8,128)(2,1)S(1)} %copy.143), channel_id=1, source_target_pairs={{16,0},{32,16},{48,32},{64,48},{80,64},{96,80},{112,96},{128,112},... | collective-permute-start | bytes 98312 | tf_op jit(solution)/shard_map/ppermute | solution.py:17
  47.5 5.5 collective-permute-start.3
  49.0 6.0 collective-permute-start.2
  56.6 14.1 %collective-permute-start.4 = (bf16[64,2,128]{2,0,1:T(8,128)(2,1)S(1)}, bf16[64,2,128]{2,0,1:T(8,128)(2,1)S(1)}, u32[]{:S(2)}, u32[]{:S(2)}) collective-permute-start(bf16[64,2,128]{2,0,1:T(8,128)(2,1)S(1)} %fusion.164), channel_id=1, source_target_pairs={{240,0},{0,16},{16,32},{32,48},{48,64},{64,80},{80,96},{96,112},{1... | collective-permute-start | bytes 98312 | tf_op jit(solution)/shard_map/ppermute | solution.py:17
  69.7 7.0 %collective-permute-start.5 = (bf16[64,2,128]{2,0,1:T(8,128)(2,1)S(1)}, bf16[64,2,128]{2,0,1:T(8,128)(2,1)S(1)}, u32[]{:S(2)}, u32[]{:S(2)}) collective-permute-start(bf16[64,2,128]{2,0,1:T(8,128)(2,1)S(1)} %fusion.164), channel_id=1, source_target_pairs={{16,0},{32,16},{48,32},{64,48},{80,64},{96,80},{112,96},{128,112},... | collective-permute-start | bytes 98312 | tf_op jit(solution)/shard_map/ppermute | solution.py:17
  77.2 36.1 %collective-permute-start.6 = (bf16[64,2,1,128]{3,0,1,2:T(8,128)(2,1)S(1)}, bf16[64,2,1,128]{3,0,1,2:T(8,128)(2,1)S(1)}, u32[]{:S(2)}, u32[]{:S(2)}) collective-permute-start(bf16[64,2,1,128]{3,0,1,2:T(8,128)(2,1)S(1)} %bitcast.1583), channel_id=1, source_target_pairs={{0,1},{1,2},{2,3},{3,4},{4,5},{5,6},{6,7},{7,8},{8,9},{9,10},{10,1... | collective-permute-start | bytes 98312 | tf_op jit(solution)/shard_map/ppermute | solution.py:28
  80.1 33.2 %collective-permute-start.7 = (bf16[64,2,1,128]{3,0,1,2:T(8,128)(2,1)S(1)}, bf16[64,2,1,128]{3,0,1,2:T(8,128)(2,1)S(1)}, u32[]{:S(2)}, u32[]{:S(2)}) collective-permute-start(bf16[64,2,1,128]{3,0,1,2:T(8,128)(2,1)S(1)} %bitcast.1584), channel_id=1, source_target_pairs={{1,0},{2,1},{3,2},{4,3},{5,4},{6,5},{7,6},{8,7},{9,8},{10,9},{11,1... | collective-permute-start | bytes 98312 | tf_op jit(solution)/shard_map/ppermute | solution.py:30
  115.8 6.5 collective-permute-start.9
  122.9 38.1 %collective-permute-start.10 = (bf16[64,2,1,128]{3,0,1,2:T(8,128)(2,1)S(1)}, bf16[64,2,1,128]{3,0,1,2:T(8,128)(2,1)S(1)}, u32[]{:S(2)}, u32[]{:S(2)}) collective-permute-start(bf16[64,2,1,128]{3,0,1,2:T(8,128)(2,1)S(1)} %bitcast.1593), channel_id=1, source_target_pairs={{0,1},{1,2},{2,3},{3,4},{4,5},{5,6},{6,7},{7,8},{8,9},{9,10},{10,1... | collective-permute-start | bytes 98312 | tf_op jit(solution)/shard_map/ppermute | solution.py:28
  125.7 35.3 %collective-permute-start.11 = (bf16[64,2,1,128]{3,0,1,2:T(8,128)(2,1)S(1)}, bf16[64,2,1,128]{3,0,1,2:T(8,128)(2,1)S(1)}, u32[]{:S(2)}, u32[]{:S(2)}) collective-permute-start(bf16[64,2,1,128]{3,0,1,2:T(8,128)(2,1)S(1)} %bitcast.1594), channel_id=1, source_target_pairs={{1,0},{2,1},{3,2},{4,3},{5,4},{6,5},{7,6},{8,7},{9,8},{10,9},{11,1... | collective-permute-start | bytes 98312 | tf_op jit(solution)/shard_map/ppermute | solution.py:30
  163.4 4.3 collective-permute-start.12
  163.5 6.8 %collective-permute-start.13 = (bf16[64,2,128]{2,0,1:T(8,128)(2,1)S(1)}, bf16[64,2,128]{2,0,1:T(8,128)(2,1)S(1)}, u32[]{:S(2)}, u32[]{:S(2)}) collective-permute-start(bf16[64,2,128]{2,0,1:T(8,128)(2,1)S(1)} %fusion.168), channel_id=1, source_target_pairs={{64,0},{80,16},{96,32},{112,48},{128,64},{144,80},{160,96},{176,11... | collective-permute-start | bytes 98312 | tf_op jit(solution)/shard_map/ppermute | solution.py:17
  170.8 36.5 %collective-permute-start.14 = (bf16[64,2,1,128]{3,0,1,2:T(8,128)(2,1)S(1)}, bf16[64,2,1,128]{3,0,1,2:T(8,128)(2,1)S(1)}, u32[]{:S(2)}, u32[]{:S(2)}) collective-permute-start(bf16[64,2,1,128]{3,0,1,2:T(8,128)(2,1)S(1)} %bitcast.1573), channel_id=1, source_target_pairs={{0,1},{1,2},{2,3},{3,4},{4,5},{5,6},{6,7},{7,8},{8,9},{9,10},{10,1... | collective-permute-start | bytes 98312 | tf_op jit(solution)/shard_map/ppermute | solution.py:28
  173.1 34.3 %collective-permute-start.15 = (bf16[64,2,1,128]{3,0,1,2:T(8,128)(2,1)S(1)}, bf16[64,2,1,128]{3,0,1,2:T(8,128)(2,1)S(1)}, u32[]{:S(2)}, u32[]{:S(2)}) collective-permute-start(bf16[64,2,1,128]{3,0,1,2:T(8,128)(2,1)S(1)} %bitcast.1574), channel_id=1, source_target_pairs={{1,0},{2,1},{3,2},{4,3},{5,4},{6,5},{7,6},{8,7},{9,8},{10,9},{11,1... | collective-permute-start | bytes 98312 | tf_op jit(solution)/shard_map/ppermute | solution.py:30
  212.9 8.3 %collective-permute-start.16 = (bf16[64,2,2,1,128]{4,0,2,1,3:T(8,128)(2,1)S(1)}, bf16[64,2,2,1,128]{4,0,2,1,3:T(8,128)(2,1)S(1)}, u32[]{:S(2)}, u32[]{:S(2)}) collective-permute-start(bf16[64,2,2,1,128]{4,0,2,1,3:T(8,128)(2,1)S(1)} %pad_maximum_fusion.40), channel_id=1, source_target_pairs={{1,0},{2,1},{3,2},{4,3},{5,4},{6,5},{7,6},{8,7},{9,8},{10,9},{11,1... | collective-permute-start | bytes 196616 | tf_op jit(solution)/shard_map/ppermute | solution.py:30
  214.5 8.4 %collective-permute-start.17 = (bf16[64,2,2,1,128]{4,0,2,1,3:T(8,128)(2,1)S(1)}, bf16[64,2,2,1,128]{4,0,2,1,3:T(8,128)(2,1)S(1)}, u32[]{:S(2)}, u32[]{:S(2)}) collective-permute-start(bf16[64,2,2,1,128]{4,0,2,1,3:T(8,128)(2,1)S(1)} %pad_maximum_fusion.40), channel_id=1, source_target_pairs={{0,1},{1,2},{2,3},{3,4},{4,5},{5,6},{6,7},{7,8},{8,9},{9,10},{10,1... | collective-permute-start | bytes 196616 | tf_op jit(solution)/shard_map/ppermute | solution.py:28
  224.5 4.3 collective-permute-start.19
  225.3 6.7 %collective-permute-start.18 = (bf16[64,2,128]{2,0,1:T(8,128)(2,1)S(1)}, bf16[64,2,128]{2,0,1:T(8,128)(2,1)S(1)}, u32[]{:S(2)}, u32[]{:S(2)}) collective-permute-start(bf16[64,2,128]{2,0,1:T(8,128)(2,1)S(1)} %get-tuple-element.48), channel_id=1, source_target_pairs={{64,0},{80,16},{96,32},{112,48},{128,64},{144,80},{160,96},{176,11... | collective-permute-start | bytes 98312 | tf_op jit(solution)/shard_map/ppermute | solution.py:17
  232.1 9.5 %collective-permute-start.20 = (bf16[64,2,2,1,128]{4,0,2,1,3:T(8,128)(2,1)S(1)}, bf16[64,2,2,1,128]{4,0,2,1,3:T(8,128)(2,1)S(1)}, u32[]{:S(2)}, u32[]{:S(2)}) collective-permute-start(bf16[64,2,2,1,128]{4,0,2,1,3:T(8,128)(2,1)S(1)} %get-tuple-element.110), channel_id=1, source_target_pairs={{1,0},{2,1},{3,2},{4,3},{5,4},{6,5},{7,6},{8,7},{9,8},{10,9},{11,1... | collective-permute-start | bytes 196616 | tf_op jit(solution)/shard_map/ppermute | solution.py:30
  236.0 5.3 collective-permute-start.21
  245.6 6.4 collective-permute-start.22
  252.2 9.0 %collective-permute-start.24 = (bf16[64,2,2,1,128]{4,0,2,1,3:T(8,128)(2,1)S(1)}, bf16[64,2,2,1,128]{4,0,2,1,3:T(8,128)(2,1)S(1)}, u32[]{:S(2)}, u32[]{:S(2)}) collective-permute-start(bf16[64,2,2,1,128]{4,0,2,1,3:T(8,128)(2,1)S(1)} %pad_maximum_fusion.42), channel_id=1, source_target_pairs={{1,0},{2,1},{3,2},{4,3},{5,4},{6,5},{7,6},{8,7},{9,8},{10,9},{11,1... | collective-permute-start | bytes 196616 | tf_op jit(solution)/shard_map/ppermute | solution.py:30
  253.8 8.9 %collective-permute-start.25 = (bf16[64,2,2,1,128]{4,0,2,1,3:T(8,128)(2,1)S(1)}, bf16[64,2,2,1,128]{4,0,2,1,3:T(8,128)(2,1)S(1)}, u32[]{:S(2)}, u32[]{:S(2)}) collective-permute-start(bf16[64,2,2,1,128]{4,0,2,1,3:T(8,128)(2,1)S(1)} %pad_maximum_fusion.42), channel_id=1, source_target_pairs={{0,1},{1,2},{2,3},{3,4},{4,5},{5,6},{6,7},{7,8},{8,9},{9,10},{10,1... | collective-permute-start | bytes 196616 | tf_op jit(solution)/shard_map/ppermute | solution.py:28
  264.3 27.8 %collective-permute-start.27 = (bf16[64,2,128]{2,0,1:T(8,128)(2,1)S(1)}, bf16[64,2,128]{2,0,1:T(8,128)(2,1)S(1)}, u32[]{:S(2)}, u32[]{:S(2)}) collective-permute-start(bf16[64,2,128]{2,0,1:T(8,128)(2,1)S(1)} %get-tuple-element.46), channel_id=1, source_target_pairs={{240,0},{0,16},{16,32},{32,48},{48,64},{64,80},{80,96},{96,112},{1... | collective-permute-start | bytes 98312 | tf_op jit(solution)/shard_map/ppermute | solution.py:17
  291.1 7.0 %collective-permute-start.26 = (bf16[64,2,128]{2,0,1:T(8,128)(2,1)S(1)}, bf16[64,2,128]{2,0,1:T(8,128)(2,1)S(1)}, u32[]{:S(2)}, u32[]{:S(2)}) collective-permute-start(bf16[64,2,128]{2,0,1:T(8,128)(2,1)S(1)} %get-tuple-element.46), channel_id=1, source_target_pairs={{16,0},{32,16},{48,32},{64,48},{80,64},{96,80},{112,96},{128,112},... | collective-permute-start | bytes 98312 | tf_op jit(solution)/shard_map/ppermute | solution.py:17
  298.2 10.1 %collective-permute-start.28 = (bf16[64,2,2,1,128]{4,0,2,1,3:T(8,128)(2,1)S(1)}, bf16[64,2,2,1,128]{4,0,2,1,3:T(8,128)(2,1)S(1)}, u32[]{:S(2)}, u32[]{:S(2)}) collective-permute-start(bf16[64,2,2,1,128]{4,0,2,1,3:T(8,128)(2,1)S(1)} %pad_maximum_fusion.43), channel_id=1, source_target_pairs={{1,0},{2,1},{3,2},{4,3},{5,4},{6,5},{7,6},{8,7},{9,8},{10,9},{11,1... | collective-permute-start | bytes 196616 | tf_op jit(solution)/shard_map/ppermute | solution.py:30
  299.9 10.6 %collective-permute-start.29 = (bf16[64,2,2,1,128]{4,0,2,1,3:T(8,128)(2,1)S(1)}, bf16[64,2,2,1,128]{4,0,2,1,3:T(8,128)(2,1)S(1)}, u32[]{:S(2)}, u32[]{:S(2)}) collective-permute-start(bf16[64,2,2,1,128]{4,0,2,1,3:T(8,128)(2,1)S(1)} %pad_maximum_fusion.43), channel_id=1, source_target_pairs={{0,1},{1,2},{2,3},{3,4},{4,5},{5,6},{6,7},{7,8},{8,9},{9,10},{10,1... | collective-permute-start | bytes 196616 | tf_op jit(solution)/shard_map/ppermute | solution.py:28
  308.3 331.8 %all-reduce.35.cloned.1.call-start = ((), (), s32[]{:S(2)}) async-start(), calls=%async_computation.1 | async-start | bytes 442368 | tf_op jit(solution)/shard_map/psum | solution.py:171
  312.1 185.7 %collective-permute-start.31 = (bf16[64,2,128]{2,0,1:T(8,128)(2,1)S(1)}, bf16[64,2,128]{2,0,1:T(8,128)(2,1)S(1)}, u32[]{:S(2)}, u32[]{:S(2)}) collective-permute-start(bf16[64,2,128]{2,0,1:T(8,128)(2,1)S(1)} %get-tuple-element.45), channel_id=1, source_target_pairs={{240,0},{0,16},{16,32},{32,48},{48,64},{64,80},{80,96},{96,112},{1... | collective-permute-start | bytes 98312 | tf_op jit(solution)/shard_map/ppermute | solution.py:17
  313.1 184.7 %collective-permute-start.30 = (bf16[64,2,128]{2,0,1:T(8,128)(2,1)S(1)}, bf16[64,2,128]{2,0,1:T(8,128)(2,1)S(1)}, u32[]{:S(2)}, u32[]{:S(2)}) collective-permute-start(bf16[64,2,128]{2,0,1:T(8,128)(2,1)S(1)} %get-tuple-element.45), channel_id=1, source_target_pairs={{16,0},{32,16},{48,32},{64,48},{80,64},{96,80},{112,96},{128,112},... | collective-permute-start | bytes 98312 | tf_op jit(solution)/shard_map/ppermute | solution.py:17
  (83 other events, 1560.2 us)
Sparse Core Ops, SparseCore 0:
  308.4 183.0 all-reduce.32
  497.9 142.1 all-reduce.34
where the time goes:
time: 651 us; the launch traced here: 649 us
  waiting for transfers between devices  264 us (41%)
  blocking collectives  216 us (33%)
  starting transfers between devices  93.6 us (14%)
  local copies, waits for them, and re-layouts  28.6 us (4%)
  between operations  16.5 us (3%)
  other arithmetic  15.3 us (2%)
  matrix products  14.9 us (2%)
    psum x1, waiting for transfers between devices, per_device(): grad_kernel = lax.psum(kernel_piece, 'phase').astype(jnp.float32)  141 us
    all_gather x4, blocking collectives, per_device(): kernel = lax.all_gather(conv_weights[block_num], 'chan', axis=3, tiled=True)  130 us
    unnamed x3, waiting for transfers between devices  91.4 us
    psum x1, blocking collectives, per_device(): grad_taps = lax.psum(jnp.stack(tap_grads), ('phase', 'chan'))  85.8 us
    ppermute x16, starting transfers between devices, shifted(): return lax.ppermute(block, axis, route)  53.4 us
    ppermute x16, waiting for transfers between devices, shifted(): return lax.ppermute(block, axis, route)  31.2 us
    ppermute x8, starting transfers between devices, padded_2(): lax.ppermute(tail, axis, [(i, (i + 1) % count) for i in range(ends)])  29.5 us
    unnamed x172, local copies, waits for them, and re-layouts  20.6 us
  transfers between devices with their start and end apart: 34, of which 15 were waited for; matrix products, arithmetic and copies ran while one was open for 4% of the time, Pallas kernels for 0%

commit v1 on v0

--- a/solution.py
+++ b/solution.py
@@ -172,7 +172,7 @@
         weight_grads[block_num] = grad_kernel
         tap_grads[block_num] = grad_tap
     grad_weights = jnp.stack(weight_grads)
-    grad_taps = lax.psum(jnp.stack(tap_grads), ("phase", "chan"))
+    grad_taps = jnp.sum(lax.all_gather(jnp.stack(tap_grads), ("phase", "chan")), axis=0)
     return (state, grad_state, grad_taps, grad_weights)
 
 

time: 651 us -> 1090 us (1.67)
  blocking collectives: 216 us -> 655 us
  waiting for transfers between devices: 264 us -> 279 us
  local copies, waits for them, and re-layouts: 28.6 us -> 15.7 us
    all_gather x0 -> x1, blocking collectives: none -> 523 us  [per_device(): lax.all_gather(jnp.stack(tap_grads), ('phase', 'chan'))]
    psum x1, waiting for transfers between devices: 141 us -> 247 us  [per_device(): grad_kernel = lax.psum(kernel_piece, 'phase').astype(jnp.float32)]
    unnamed x3, waiting for transfers between devices: 91.4 us -> 0.03 us
    psum x1 -> x0, blocking collectives: 85.8 us -> none  [per_device(): grad_taps = lax.psum(jnp.stack(tap_grads), ('phase', 'chan'))]
    unnamed x172 -> x170, local copies, waits for them, and re-layouts: 20.6 us -> 6.78 us
  transfers between devices with their start and end apart: 34 -> 34, of which waited for: 15 -> 14; matrix products, arithmetic and copies ran while one was open for 4% -> 3% of each run, Pallas kernels for 0% -> 0%
where the time goes in v1:
time: 1090 us
  blocking collectives  655 us (60%)
  waiting for transfers between devices  279 us (26%)
  starting transfers between devices  92.3 us (8%)
  other arithmetic  19.1 us (2%)
  between operations  16.8 us (2%)
  local copies, waits for them, and re-layouts  15.7 us (1%)
  matrix products  14.8 us (1%)
    all_gather x1, blocking collectives, per_device(): lax.all_gather(jnp.stack(tap_grads), ('phase', 'chan'))  523 us
    psum x1, waiting for transfers between devices, per_device(): grad_kernel = lax.psum(kernel_piece, 'phase').astype(jnp.float32)  247 us
    all_gather x4, blocking collectives, per_device(): kernel = lax.all_gather(conv_weights[block_num], 'chan', axis=3, tiled=True)  131 us
    ppermute x16, starting transfers between devices, shifted(): return lax.ppermute(block, axis, route)  54.2 us
    ppermute x16, waiting for transfers between devices, shifted(): return lax.ppermute(block, axis, route)  31.7 us
    ppermute x8, starting transfers between devices, padded_2(): lax.ppermute(tail, axis, [(i, (i + 1) % count) for i in range(ends)])  27.7 us
  transfers between devices with their start and end apart: 34, of which 14 were waited for; matrix products, arithmetic and copies ran while one was open for 3% of the time, Pallas kernels for 0%

profile of v1, /device:TPU:7, one launch (start us, length us, event | category | flops | bytes accessed | tf_op | source)
XLA Modules:
  0.0 1092.8 jit_solution(2123093030799779049)
XLA Ops:
  8.0 3.4 collective-permute-start
  12.5 34.2 %all-gather = bf16[1,64,27,2,64]{1,3,2,0,4:T(2,128)(2,1)S(1)} all-gather(bf16[1,64,27,2,4]{1,3,2,0,4:T(2,128)(2,1)S(1)} %copy.557), channel_id=2, replica_groups=mesh['phase'=16,'chan'=16] {'chan'}, dimensions={4}, use_global_device_ids=true | all-gather | bytes 470016 | tf_op jit(solution)/shard_map/all_gather | solution.py:109
  49.7 4.0 collective-permute-start.2
  56.4 13.0 %collective-permute-start.4 = (bf16[64,2,128]{2,0,1:T(8,128)(2,1)S(1)}, bf16[64,2,128]{2,0,1:T(8,128)(2,1)S(1)}, u32[]{:S(2)}, u32[]{:S(2)}) collective-permute-start(bf16[64,2,128]{2,0,1:T(8,128)(2,1)S(1)} %fusion.164), channel_id=1, source_target_pairs={{240,0},{0,16},{16,32},{32,48},{48,64},{64,80},{80,96},{96,112},{1... | collective-permute-start | bytes 98312 | tf_op jit(solution)/shard_map/ppermute | solution.py:17
  70.5 5.9 collective-permute-done.5
  76.5 3.3 collective-permute-start.6
  79.8 1.3 collective-permute-start.7
  81.1 31.8 %all-gather.1 = bf16[1,64,27,2,64]{1,3,2,0,4:T(2,128)(2,1)S(1)} all-gather(bf16[1,64,27,2,4]{1,3,2,0,4:T(2,128)(2,1)S(1)} %copy.558), channel_id=3, replica_groups=mesh['phase'=16,'chan'=16] {'chan'}, dimensions={4}, use_global_device_ids=true | all-gather | bytes 470016 | tf_op jit(solution)/shard_map/all_gather | solution.py:109
  115.1 1.5 collective-permute-start.9
  117.9 3.7 collective-permute-done.9
  122.2 2.6 collective-permute-start.10
  124.8 1.3 collective-permute-start.11
  126.2 32.6 %all-gather.2 = bf16[1,64,27,2,64]{1,3,2,0,4:T(2,128)(2,1)S(1)} all-gather(bf16[1,64,27,2,4]{1,3,2,0,4:T(2,128)(2,1)S(1)} %copy.559), channel_id=4, replica_groups=mesh['phase'=16,'chan'=16] {'chan'}, dimensions={4}, use_global_device_ids=true | all-gather | bytes 470016 | tf_op jit(solution)/shard_map/all_gather | solution.py:109
  161.0 3.0 collective-permute-start.13
  165.3 2.6 collective-permute-done.13
  168.0 1.3 collective-permute-start.14
  170.6 32.9 %all-gather.3 = bf16[1,64,27,2,64]{1,3,2,0,4:T(2,128)(2,1)S(1)} all-gather(bf16[1,64,27,2,4]{1,3,2,0,4:T(2,128)(2,1)S(1)} %copy.560), channel_id=5, replica_groups=mesh['phase'=16,'chan'=16] {'chan'}, dimensions={4}, use_global_device_ids=true | all-gather | bytes 470016 | tf_op jit(solution)/shard_map/all_gather | solution.py:109
  212.5 4.0 collective-permute-start.17
  222.5 2.6 collective-permute-start.18
  226.4 2.7 collective-permute-done.18
  231.8 4.0 collective-permute-start.21
  242.6 4.8 collective-permute-done.22
  249.1 4.0 collective-permute-start.25
  257.8 27.6 %collective-permute-start.27 = (bf16[64,2,128]{2,0,1:T(8,128)(2,1)S(1)}, bf16[64,2,128]{2,0,1:T(8,128)(2,1)S(1)}, u32[]{:S(2)}, u32[]{:S(2)}) collective-permute-start(bf16[64,2,128]{2,0,1:T(8,128)(2,1)S(1)} %get-tuple-element.46), channel_id=1, source_target_pairs={{240,0},{0,16},{16,32},{32,48},{48,64},{64,80},{80,96},{96,112},{1... | collective-permute-start | bytes 98312 | tf_op jit(solution)/shard_map/ppermute | solution.py:17
  286.4 5.9 collective-permute-done.26
  294.1 4.6 collective-permute-start.29
  305.1 523.3 %all-gather.4 = f32[1024,3,64]{2,1,0:T(4,128)S(1)} all-gather(f32[4,3,64]{2,1,0:T(4,128)S(1)} %pad_maximum_fusion.48), channel_id=6, replica_groups=mesh['phase'=16,'chan'=16] {'phase','chan'}, dimensions={0}, use_global_device_ids=true | all-gather | bytes 789504 | tf_op jit(solution)/shard_map/all_gather | solution.py:175
  829.5 1.5 dynamic-slice_bitcast_fusion
  831.1 1.6 dynamic-slice_bitcast_fusion.1
  832.6 1.5 dynamic-slice_bitcast_fusion.2
  834.2 1.6 dynamic-slice_bitcast_fusion.3
  836.6 247.4 %all-reduce.35.cloned.1.call-done = (bf16[1,64,27,2,4]{1,4,2,3,0:T(4,128)(2,1)}, bf16[1,64,27,2,4]{1,4,2,3,0:T(4,128)(2,1)}, bf16[1,64,27,2,4]{1,4,2,3,0:T(4,128)(2,1)}, bf16[1,64,27,2,4]{1,4,2,3,0:T(4,128)(2,1)}) async-done(((bf16[1,64,27,2,4]{1,4,2,3,0:T(4,128)(2,1)}, bf16[1,64,27,2,4]{1,4,2,3,0:T(4,128)(2,1)}, bf16[1,64,27,2,4]{1,4,2,3,0:T(4,128)(2,1)}, bf16[1,64,27,2,4]{1,4,2,3,0:T(4,128)(2,1)}), ...) | async-done | bytes 110608 | tf_op jit(solution)/shard_map/psum | solution.py:171
  (388 shorter events, 60.6 us)
Async XLA Ops:
  7.2 822.4 %all-reduce.33.cloned.1.call-start = ((), (), s32[]{:S(2)}) async-start(), calls=%async_computation | async-start | bytes 7077888
  8.0 39.8 %collective-permute-start = (bf16[64,2,128]{2,0,1:T(8,128)(2,1)S(1)}, bf16[64,2,128]{2,0,1:T(8,128)(2,1)S(1)}, u32[]{:S(2)}, u32[]{:S(2)}) collective-permute-start(bf16[64,2,128]{2,0,1:T(8,128)(2,1)S(1)} %copy.142), channel_id=1, source_target_pairs={{240,0},{0,16},{16,32},{32,48},{48,64},{64,80},{80,96},{96,112},{1... | collective-permute-start | bytes 98312 | tf_op jit(solution)/shard_map/ppermute | solution.py:17
  11.4 36.4 %collective-permute-start.1 = (bf16[64,2,128]{2,0,1:T(8,128)(2,1)S(1)}, bf16[64,2,128]{2,0,1:T(8,128)(2,1)S(1)}, u32[]{:S(2)}, u32[]{:S(2)}) collective-permute-start(bf16[64,2,128]{2,0,1:T(8,128)(2,1)S(1)} %copy.142), channel_id=1, source_target_pairs={{16,0},{32,16},{48,32},{64,48},{80,64},{96,80},{112,96},{128,112},... | collective-permute-start | bytes 98312 | tf_op jit(solution)/shard_map/ppermute | solution.py:17
  48.2 5.5 collective-permute-start.3
  49.7 5.6 collective-permute-start.2
  56.4 14.1 %collective-permute-start.4 = (bf16[64,2,128]{2,0,1:T(8,128)(2,1)S(1)}, bf16[64,2,128]{2,0,1:T(8,128)(2,1)S(1)}, u32[]{:S(2)}, u32[]{:S(2)}) collective-permute-start(bf16[64,2,128]{2,0,1:T(8,128)(2,1)S(1)} %fusion.164), channel_id=1, source_target_pairs={{240,0},{0,16},{16,32},{32,48},{48,64},{64,80},{80,96},{96,112},{1... | collective-permute-start | bytes 98312 | tf_op jit(solution)/shard_map/ppermute | solution.py:17
  69.5 7.0 collective-permute-start.5
  76.5 36.6 %collective-permute-start.6 = (bf16[64,2,1,128]{3,0,1,2:T(8,128)(2,1)S(1)}, bf16[64,2,1,128]{3,0,1,2:T(8,128)(2,1)S(1)}, u32[]{:S(2)}, u32[]{:S(2)}) collective-permute-start(bf16[64,2,1,128]{3,0,1,2:T(8,128)(2,1)S(1)} %bitcast.1585), channel_id=1, source_target_pairs={{0,1},{1,2},{2,3},{3,4},{4,5},{5,6},{6,7},{7,8},{8,9},{9,10},{10,1... | collective-permute-start | bytes 98312 | tf_op jit(solution)/shard_map/ppermute | solution.py:28
  79.8 33.3 %collective-permute-start.7 = (bf16[64,2,1,128]{3,0,1,2:T(8,128)(2,1)S(1)}, bf16[64,2,1,128]{3,0,1,2:T(8,128)(2,1)S(1)}, u32[]{:S(2)}, u32[]{:S(2)}) collective-permute-start(bf16[64,2,1,128]{3,0,1,2:T(8,128)(2,1)S(1)} %bitcast.1586), channel_id=1, source_target_pairs={{1,0},{2,1},{3,2},{4,3},{5,4},{6,5},{7,6},{8,7},{9,8},{10,9},{11,1... | collective-permute-start | bytes 98312 | tf_op jit(solution)/shard_map/ppermute | solution.py:30
  115.1 6.5 collective-permute-start.9
  122.2 36.8 %collective-permute-start.10 = (bf16[64,2,1,128]{3,0,1,2:T(8,128)(2,1)S(1)}, bf16[64,2,1,128]{3,0,1,2:T(8,128)(2,1)S(1)}, u32[]{:S(2)}, u32[]{:S(2)}) collective-permute-start(bf16[64,2,1,128]{3,0,1,2:T(8,128)(2,1)S(1)} %bitcast.1595), channel_id=1, source_target_pairs={{0,1},{1,2},{2,3},{3,4},{4,5},{5,6},{6,7},{7,8},{8,9},{9,10},{10,1... | collective-permute-start | bytes 98312 | tf_op jit(solution)/shard_map/ppermute | solution.py:28
  124.8 34.1 %collective-permute-start.11 = (bf16[64,2,1,128]{3,0,1,2:T(8,128)(2,1)S(1)}, bf16[64,2,1,128]{3,0,1,2:T(8,128)(2,1)S(1)}, u32[]{:S(2)}, u32[]{:S(2)}) collective-permute-start(bf16[64,2,1,128]{3,0,1,2:T(8,128)(2,1)S(1)} %bitcast.1596), channel_id=1, source_target_pairs={{1,0},{2,1},{3,2},{4,3},{5,4},{6,5},{7,6},{8,7},{9,8},{10,9},{11,1... | collective-permute-start | bytes 98312 | tf_op jit(solution)/shard_map/ppermute | solution.py:30
  160.9 4.3 collective-permute-start.12
  161.0 6.9 collective-permute-start.13
  168.0 37.7 %collective-permute-start.14 = (bf16[64,2,1,128]{3,0,1,2:T(8,128)(2,1)S(1)}, bf16[64,2,1,128]{3,0,1,2:T(8,128)(2,1)S(1)}, u32[]{:S(2)}, u32[]{:S(2)}) collective-permute-start(bf16[64,2,1,128]{3,0,1,2:T(8,128)(2,1)S(1)} %bitcast.1575), channel_id=1, source_target_pairs={{0,1},{1,2},{2,3},{3,4},{4,5},{5,6},{6,7},{7,8},{8,9},{9,10},{10,1... | collective-permute-start | bytes 98312 | tf_op jit(solution)/shard_map/ppermute | solution.py:28
  169.3 36.4 %collective-permute-start.15 = (bf16[64,2,1,128]{3,0,1,2:T(8,128)(2,1)S(1)}, bf16[64,2,1,128]{3,0,1,2:T(8,128)(2,1)S(1)}, u32[]{:S(2)}, u32[]{:S(2)}) collective-permute-start(bf16[64,2,1,128]{3,0,1,2:T(8,128)(2,1)S(1)} %bitcast.1576), channel_id=1, source_target_pairs={{1,0},{2,1},{3,2},{4,3},{5,4},{6,5},{7,6},{8,7},{9,8},{10,9},{11,1... | collective-permute-start | bytes 98312 | tf_op jit(solution)/shard_map/ppermute | solution.py:30
  210.9 8.3 collective-permute-start.16
  212.5 8.4 collective-permute-start.17
  222.0 4.4 collective-permute-start.19
  222.5 6.7 collective-permute-start.18
  229.3 8.0 collective-permute-start.20
  231.8 5.3 collective-permute-start.21
  241.0 6.4 collective-permute-start.22
  247.6 7.6 collective-permute-start.24
  249.1 7.6 collective-permute-start.25
  257.8 28.6 %collective-permute-start.27 = (bf16[64,2,128]{2,0,1:T(8,128)(2,1)S(1)}, bf16[64,2,128]{2,0,1:T(8,128)(2,1)S(1)}, u32[]{:S(2)}, u32[]{:S(2)}) collective-permute-start(bf16[64,2,128]{2,0,1:T(8,128)(2,1)S(1)} %get-tuple-element.46), channel_id=1, source_target_pairs={{240,0},{0,16},{16,32},{32,48},{48,64},{64,80},{80,96},{96,112},{1... | collective-permute-start | bytes 98312 | tf_op jit(solution)/shard_map/ppermute | solution.py:17
  285.4 7.0 collective-permute-start.26
  292.5 8.3 collective-permute-start.28
  294.1 9.0 collective-permute-start.29
  300.8 783.2 %all-reduce.35.cloned.1.call-start = ((), (), s32[]{:S(2)}) async-start(), calls=%async_computation.1 | async-start | bytes 442368 | tf_op jit(solution)/shard_map/psum | solution.py:171
  304.1 531.7 %collective-permute-start.31 = (bf16[64,2,128]{2,0,1:T(8,128)(2,1)S(1)}, bf16[64,2,128]{2,0,1:T(8,128)(2,1)S(1)}, u32[]{:S(2)}, u32[]{:S(2)}) collective-permute-start(bf16[64,2,128]{2,0,1:T(8,128)(2,1)S(1)} %get-tuple-element.45), channel_id=1, source_target_pairs={{240,0},{0,16},{16,32},{32,48},{48,64},{64,80},{80,96},{96,112},{1... | collective-permute-start | bytes 98312 | tf_op jit(solution)/shard_map/ppermute | solution.py:17
  305.1 530.7 %collective-permute-start.30 = (bf16[64,2,128]{2,0,1:T(8,128)(2,1)S(1)}, bf16[64,2,128]{2,0,1:T(8,128)(2,1)S(1)}, u32[]{:S(2)}, u32[]{:S(2)}) collective-permute-start(bf16[64,2,128]{2,0,1:T(8,128)(2,1)S(1)} %get-tuple-element.45), channel_id=1, source_target_pairs={{16,0},{32,16},{48,32},{64,48},{80,64},{96,80},{112,96},{128,112},... | collective-permute-start | bytes 98312 | tf_op jit(solution)/shard_map/ppermute | solution.py:17
  (82 other events, 3763.6 us)
Sparse Core Ops, SparseCore 0:
  300.9 195.4 all-reduce.32
  835.9 248.0 all-reduce.34
